TPU v7x, 256 devices: a whole 4x4x8 slice. The times are simulated.
256 devices in a mesh: row: 128 (over z, y_lo, x, core), ch: 2 (over y_hi).
Axes of the slice: x: 4, y: 4 (y_hi: 2, y_lo: 2; y = y_hi * 2 + y_lo), z: 8, core: 2. Of those that a mesh axis runs over, the one named last changes fastest.
Arguments:
- pair_rep: bfloat16 [384, 384, 128], P('row'), may hold values from -6 to 6
- res_mask: int32 [384], replicated, may hold values 0 or 1
- in_gain: float32 [128], replicated, may hold values from 0.5 to 1.5
- w_left: bfloat16 [128, 128], P(None, 'ch'), may hold values from -0.5 to 0.5
- w_left_gate: bfloat16 [128, 128], P(None, 'ch'), may hold values from -0.5 to 0.5
- w_right: bfloat16 [128, 128], P(None, 'ch'), may hold values from -0.5 to 0.5
- w_right_gate: bfloat16 [128, 128], P(None, 'ch'), may hold values from -0.5 to 0.5
- w_gate: bfloat16 [128, 128], replicated, may hold values from -0.5 to 0.5
- mid_gain: float32 [128], replicated, may hold values from 0.5 to 1.5
- w_out: bfloat16 [128, 128], replicated, may hold values from -0.5 to 0.5
- next_gain: float32 [128], replicated, may hold values from 0.5 to 1.5
Outputs:
- new_pair: bfloat16 [384, 384, 128], P(None, 'row', 'ch')
- new_norm: bfloat16 [384, 384, 128], P(None, 'row', 'ch')
All inputs are finite; a program needn't handle non-finite values.
Results may differ from a plain program's by a relative error of at most 0.0065.
Values may be sent and summed in bfloat16 or wider, within the bound.
A program may use at most 64 MiB of HBM per device.

v0:
```python
import jax
import jax.numpy as jnp
from jax import lax
from jax.sharding import Mesh
from jax.sharding import PartitionSpec as P

ROW = ("row_0", "row_1", "row_2", "row_3")


epsilon = 1e-05


def split_up(array, dim, devices):
    dims = array.shape
    blocks = array.reshape(*dims[:dim], devices, dims[dim] // devices, *dims[dim + 1 :])
    return jnp.moveaxis(blocks, dim, 0)


def in_order(blocks, dim):
    dims = list(blocks.shape[1:])
    dims[dim] *= blocks.shape[0]
    return jnp.moveaxis(blocks, 0, dim).reshape(dims)


def moved_by_axis(blocks, axes, order):
    inside = blocks.shape[1:]
    whole = blocks.reshape(*(lax.axis_size(a) for a in axes), *inside)
    for k in order:
        whole = lax.all_to_all(whole, axes[k], k, k, tiled=True)
    return whole.reshape(-1, *inside)


def exchange_by_chip(array, groups, order, split_dim, concat_dim):
    devices = lax.axis_size(groups[0]) * lax.axis_size(groups[1])
    blocks = split_up(array, split_dim, devices)
    return in_order(moved_by_axis(blocks, groups, order), concat_dim)


def copy_for_each(array, axis):
    copies = jnp.broadcast_to(array, (lax.axis_size(axis), *array.shape))
    return lax.all_to_all(copies, axis, split_axis=0, concat_axis=0, tiled=True)


def over_copies(array, axis):
    return copy_for_each(array, axis).sum(axis=0)


def together(arrays, axis):
    vector, at, gathered = (jnp.concatenate([a.reshape(-1) for a in arrays]), 0, [])
    so_far = over_copies(vector, axis)
    for a in arrays:
        gathered.append(so_far[at : at + a.size].reshape(a.shape))
        at += a.size
    return tuple(gathered)


def sum_at_owner(array, axis, dim):
    blocks = split_up(array, dim, lax.axis_size(axis))
    arrived = lax.all_to_all(blocks, axis, split_axis=0, concat_axis=0, tiled=True)
    return arrived.astype(jnp.float32).sum(axis=0)


def packed_total(arrays, axis):
    vector, at, gathered = (jnp.concatenate([a.reshape(-1) for a in arrays]), 0, [])
    so_far = lax.psum(vector, axis)
    for a in arrays:
        gathered.append(so_far[at : at + a.size].reshape(a.shape))
        at += a.size
    return tuple(gathered)


def normalize(values, scale_gain, along):
    values = values.astype(jnp.float32)
    average = jnp.mean(values, along, keepdims=True)
    centred = values - average
    spread = jnp.mean(centred * centred, along, keepdims=True)
    return centred * lax.rsqrt(spread + epsilon) * scale_gain


def gated(normed, weight, weight_gate, pair_mask):
    values_lin = jnp.einsum("ilc,ch->hil", normed, weight, preferred_element_type=jnp.float32)
    switch = jnp.einsum("ilc,ch->hil", normed, weight_gate, preferred_element_type=jnp.float32)
    return (jax.nn.sigmoid(switch) * values_lin * pair_mask[None]).astype(jnp.bfloat16)


def batched_rows(first, second):
    return lax.dot_general(
        first, second, (((2,), (2,)), ((0,), (0,))), preferred_element_type=jnp.float32
    )


def local(
    pair_rep,
    res_mask,
    in_gain,
    w_left,
    w_left_gate,
    w_right,
    w_right_gate,
    w_gate,
    mid_gain,
    w_out,
    next_gain,
):
    row_count = pair_rep.shape[0]
    channels = pair_rep.shape[2]
    hid_local = w_left.shape[1]
    ch_count = lax.axis_size("ch")
    ch_index = lax.axis_index("ch")
    row_index = lax.axis_index(ROW)
    ch_width = channels // ch_count
    res_float = res_mask.astype(jnp.float32)
    own_mask = lax.dynamic_slice_in_dim(res_float, row_index * row_count, row_count)
    pair_mask = own_mask[:, None] * res_float[None, :]
    normed = normalize(pair_rep, in_gain, 2).astype(jnp.bfloat16)
    left_side = gated(normed, w_left, w_left_gate, pair_mask)
    right_side = gated(normed, w_right, w_right_gate, pair_mask)
    pair_here = exchange_by_chip(pair_rep, (("row_0", "row_1", "row_2"), "row_3"), (1, 0), 1, 0)
    normed_here = normalize(pair_here, in_gain, 2).astype(jnp.bfloat16)
    triangle = batched_rows(right_side, lax.all_gather(left_side, ROW, axis=1, tiled=True))
    einsum_form = "kba,kc->abc"
    hidden_total = hid_local * ch_count
    stat_sums = together((jnp.sum(triangle, 0), jnp.sum(triangle * triangle, 0)), "ch")
    mean_vals = stat_sums[0] / hidden_total
    var_vals = stat_sums[1] / hidden_total - mean_vals * mean_vals
    own_gain = lax.dynamic_slice_in_dim(mid_gain, ch_index * hid_local, hid_local)
    tri_normed = (
        (triangle - mean_vals) * lax.rsqrt(var_vals + epsilon) * own_gain[:, None, None]
    ).astype(jnp.bfloat16)
    w_rows = lax.dynamic_slice_in_dim(w_out, ch_index * hid_local, hid_local, 0)
    partial_terms = jnp.einsum(einsum_form, tri_normed, w_rows, preferred_element_type=jnp.float32)
    update = sum_at_owner(partial_terms.astype(jnp.bfloat16), "ch", 2)
    w_cols = lax.dynamic_slice_in_dim(w_gate, ch_index * ch_width, ch_width, 1)
    gate_vals = jax.nn.sigmoid(
        jnp.einsum("abc,cd->abd", normed_here, w_cols, preferred_element_type=jnp.float32)
    )
    pair_half = lax.dynamic_slice_in_dim(pair_here, ch_index * ch_width, ch_width, 2)
    new_half = (pair_half.astype(jnp.float32) + gate_vals * update).astype(jnp.bfloat16)
    values = new_half.astype(jnp.float32)
    next_sums = packed_total((jnp.sum(values, 2), jnp.sum(values * values, 2)), "ch")
    next_mean = next_sums[0] / channels
    next_var = next_sums[1] / channels - next_mean * next_mean
    own_next = lax.dynamic_slice_in_dim(next_gain, ch_index * ch_width, ch_width)
    norm_half = (
        (values - next_mean[..., None]) * lax.rsqrt(next_var + epsilon)[..., None] * own_next
    ).astype(jnp.bfloat16)
    return (new_half, norm_half)


def solution(mesh):
    split = Mesh(
        mesh.devices.reshape(8, 2, 4, 2, mesh.shape["ch"]),
        ("row_0", "row_1", "row_2", "row_3", "ch"),
    )
    return jax.shard_map(
        local,
        mesh=split,
        in_specs=(
            P(ROW, None, None),
            P(),
            P(),
            P(None, "ch"),
            P(None, "ch"),
            P(None, "ch"),
            P(None, "ch"),
            P(),
            P(),
            P(),
            P(),
        ),
        out_specs=(P(None, ROW, "ch"), P(None, ROW, "ch")),
        check_vma=False,
    )
```

profile of v0, /device:TPU:1, one launch (start us, length us, event | category | flops | bytes accessed | tf_op | source)
XLA Modules:
  0.0 317.5 jit_solution(7978292074478839061)
XLA Ops:
  8.1 1.1 convert_reduce_fusion
  9.2 1.4 fusion.22
  10.6 1.5 fusion.6
  12.2 2.2 fusion.18
  14.4 1.3 reshape.148
  15.8 6.8 %all_to_all.21 = bf16[64,2,3,3,128]{4,0,3,2,1:T(8,128)(2,1)S(1)} all-to-all(bf16[64,2,3,3,128]{4,0,3,2,1:T(8,128)(2,1)S(1)} %copy.83), channel_id=1, replica_groups=mesh['row_0'=8,'row_1'=2,'row_2'=4,'row_3'=2,'ch'=2] {'row_3'}, dimensions={1} | all-to-all | bytes 589824 | tf_op jit(solution)/shard_map/all_to_all | solution.py:29
  22.5 1.0 copy.84
  23.6 11.0 %all-to-all-start.1 = ((bf16[64,2,3,3,128]{4,1,3,2,0:T(2,128)(2,1)}), bf16[64,2,3,3,128]{4,1,3,2,0:T(2,128)(2,1)S(1)}, u32[]{:S(2)}, u32[]{:S(2)}) async-start(bf16[64,2,3,3,128]{4,1,3,2,0:T(2,128)(2,1)} %copy.84), calls=%async_computation.1 | async-start | bytes 589824 | tf_op jit(solution)/shard_map/all_to_all | solution.py:29
  36.0 1.5 fusion.9
  37.5 1.5 fusion.19
  39.0 8.2 %all-to-all-done.1 = bf16[64,2,3,3,128]{4,1,3,2,0:T(2,128)(2,1)S(1)} async-done(((bf16[64,2,3,3,128]{4,1,3,2,0:T(2,128)(2,1)}), bf16[64,2,3,3,128]{4,1,3,2,0:T(2,128)(2,1)S(1)}, u32[]{:S(2)}, u32[]{:S(2)}) %all-to-all-start.1) | async-done | bytes 294944 | tf_op jit(solution)/shard_map/all_to_all | solution.py:29
  47.7 0.9 convert_reduce_fusion.1
  48.7 1.7 fusion.26
  50.4 202.7 %all-gather.2.cloned.1.call-done = bf16[64,384,384]{2,0,1:T(8,128)(2,1)} async-done(((bf16[64,3,384]{2,0,1:T(8,128)(2,1)}), bf16[64,384,384]{2,0,1:T(8,128)(2,1)}) %all-gather.2.cloned.1.call-update) | async-done | bytes 18874384 | tf_op jit(solution)/shard_map/all_gather | solution.py:120
  253.1 29.4 %fusion.50 = (f32[3,384]{1,0:T(4,128)S(1)}, f32[3,384]{1,0:T(4,128)S(1)}, f32[64,3,384]{2,1,0:T(4,128)S(1)}) fusion(bf16[64,384,384]{2,0,1:T(8,128)(2,1)} %all-gather.2.cloned.1.call-done, bf16[64,3,384]{2,0,1:T(8,128)(2,1)S(1)} %fusion.19), kind=kOutput, calls=%fused_computation.78 | convolution fusion | flops 56841984 | bytes 19325952 | tf_op jit(solution)/shard_map/dot_general | solution.py:87
  283.4 3.2 %all-to-all-start.2 = ((f32[2,1,2304]{2,1,0:T(1,128)}), f32[2,1,2304]{2,1,0:T(1,128)S(1)}, u32[]{:S(2)}, u32[]{:S(2)}) async-start(f32[2,1,2304]{2,1,0:T(1,128)} %broadcast_in_dim.2), calls=%async_computation.2 | async-start | bytes 36864 | tf_op jit(solution)/shard_map/all_to_all | solution.py:41
  286.8 1.3 copy.88
  288.3 2.6 all-to-all-done.2
  291.4 0.7 copy.124
  292.1 3.4 %all-to-all-start.3 = ((bf16[2,384,3,64]{1,3,2,0:T(8,128)(2,1)}), bf16[2,384,3,64]{1,3,2,0:T(8,128)(2,1)S(1)}, u32[]{:S(2)}, u32[]{:S(2)}) async-start(bf16[2,384,3,64]{1,3,2,0:T(8,128)(2,1)} %bitcast.39), calls=%async_computation.3 | async-start | bytes 589824 | tf_op jit(solution)/shard_map/all_to_all | solution.py:59
  295.7 1.3 copy.91
  297.5 3.8 %all-to-all-done.3 = bf16[2,384,3,64]{1,3,2,0:T(8,128)(2,1)S(1)} async-done(((bf16[2,384,3,64]{1,3,2,0:T(8,128)(2,1)}), bf16[2,384,3,64]{1,3,2,0:T(8,128)(2,1)S(1)}, u32[]{:S(2)}, u32[]{:S(2)}) %all-to-all-start.3) | async-done | bytes 294944 | tf_op jit(solution)/shard_map/all_to_all | solution.py:59
  302.7 6.5 %psum.7 = f32[2304]{0:T(1024)S(1)} all-reduce(f32[2304]{0:T(1024)S(1)} %pad_maximum_fusion.1), channel_id=1, replica_groups=mesh['row_0'=8,'row_1'=2,'row_2'=4,'row_3'=2,'ch'=2] {'ch'}, use_global_device_ids=true, to_apply=%region_10.0 | all-reduce | flops 2304 | bytes 18432 | tf_op jit(solution)/shard_map/psum | solution.py:65
  309.8 0.8 fusion.30
  (50 shorter events, 7.3 us)
Async XLA Ops:
  7.2 283.9 %copy-start = (bf16[128,128]{1,0:T(8,128)(2,1)S(1)}, bf16[128,128]{1,0:T(8,128)(2,1)}, u32[]{:S(2)}) copy-start(bf16[128,128]{1,0:T(8,128)(2,1)} %param.20) | copy-start | bytes 98308
  7.2 245.9 %all-gather.2.cloned.1.call-start = ((), (), s32[]{:S(2)}) async-start(), calls=%async_computation.4 | async-start | bytes 19021824 | tf_op jit(solution)/shard_map/all_gather | solution.py:120
  12.1 289.2 %copy-start.2 = (bf16[128,128]{1,0:T(8,128)(2,1)S(1)}, bf16[128,128]{1,0:T(8,128)(2,1)}, u32[]{:S(2)}) copy-start(bf16[128,128]{1,0:T(8,128)(2,1)} %param.18) | copy-start | bytes 98308
  12.1 289.2 %copy-start.3 = (f32[128]{0:T(128)S(1)}, f32[128]{0:T(128)}, u32[]{:S(2)}) copy-start(f32[128]{0:T(128)} %param.13) | copy-start | bytes 1540
  23.6 23.7 %all-to-all-start.1 = ((bf16[64,2,3,3,128]{4,1,3,2,0:T(2,128)(2,1)}), bf16[64,2,3,3,128]{4,1,3,2,0:T(2,128)(2,1)S(1)}, u32[]{:S(2)}, u32[]{:S(2)}) async-start(bf16[64,2,3,3,128]{4,1,3,2,0:T(2,128)(2,1)} %copy.84), calls=%async_computation.1 | async-start | bytes 589824 | tf_op jit(solution)/shard_map/all_to_all | solution.py:29
  283.4 7.5 %all-to-all-start.2 = ((f32[2,1,2304]{2,1,0:T(1,128)}), f32[2,1,2304]{2,1,0:T(1,128)S(1)}, u32[]{:S(2)}, u32[]{:S(2)}) async-start(f32[2,1,2304]{2,1,0:T(1,128)} %broadcast_in_dim.2), calls=%async_computation.2 | async-start | bytes 36864 | tf_op jit(solution)/shard_map/all_to_all | solution.py:41
  292.1 9.1 %all-to-all-start.3 = ((bf16[2,384,3,64]{1,3,2,0:T(8,128)(2,1)}), bf16[2,384,3,64]{1,3,2,0:T(8,128)(2,1)S(1)}, u32[]{:S(2)}, u32[]{:S(2)}) async-start(bf16[2,384,3,64]{1,3,2,0:T(8,128)(2,1)} %bitcast.39), calls=%async_computation.3 | async-start | bytes 589824 | tf_op jit(solution)/shard_map/all_to_all | solution.py:59
  302.0 8.6 %copy-start.1 = (bf16[384,3,64]{0,2,1:T(8,128)(2,1)}, bf16[384,3,64]{0,2,1:T(8,128)(2,1)S(1)}, u32[]{:S(2)}) copy-start(bf16[384,3,64]{0,2,1:T(8,128)(2,1)S(1)} %get-tuple-element.11) | copy-start | bytes 442372
Sparse Core Ops, SparseCore 0:
  14.5 238.5 all-gather.1
where the time goes:
time: 322 us; the launch traced here: 317 us
  waiting for transfers between devices  217 us (67%)
  matrix products  37 us (11%)
  starting transfers between devices  17.7 us (5%)
  between operations  14.3 us (4%)
  blocking collectives  13.3 us (4%)
  local copies, waits for them, and re-layouts  10.5 us (3%)
  other arithmetic  7.41 us (2%)
    all_gather x1, waiting for transfers between devices, local(): lax.all_gather(left_side, ROW, axis=1, tiled=True)  203 us
    dot_general x1, matrix products, batched_rows(): lax.dot_general(first, second, (((2,), (2,)), ((0,), (0,))), preferred_el...  29.4 us
    all_to_all x1, starting transfers between devices, moved_by_axis(): whole = lax.all_to_all(whole, axes[k], k, k, tiled=True)  11 us
    all_to_all x1, waiting for transfers between devices, moved_by_axis(): whole = lax.all_to_all(whole, axes[k], k, k, tiled=True)  8.24 us
    all_to_all x1, blocking collectives, moved_by_axis(): whole = lax.all_to_all(whole, axes[k], k, k, tiled=True)  6.79 us
    psum x1, blocking collectives, packed_total(): so_far = lax.psum(vector, axis)  6.48 us
  transfers between devices with their start and end apart: 4, of which 4 were waited for; matrix products, arithmetic and copies ran while one was open for 4% of the time, Pallas kernels for 0%

commit v1 on v0

v1 whole, which is shorter than its diff:
```python
import functools

import jax
import jax.numpy as jnp
from jax import lax
from jax.experimental import pallas as pl
from jax.experimental.pallas import tpu as pltpu
from jax.sharding import PartitionSpec as P

EPS = 1e-05
F32 = jnp.float32
BF16 = jnp.bfloat16
GROUPS = 4


def dot(a, b, ca, cb):
    return lax.dot_general(a, b, (((ca,), (cb,)), ((), ())), preferred_element_type=F32)


def iota(shape, dim):
    return lax.broadcasted_iota(jnp.int32, shape, dim)


def one_hot(cond):
    return jnp.where(cond, 1.0, 0.0).astype(BF16)


def normalize(v, gain):
    scale = 1.0 / v.shape[1]
    centred = v - jnp.sum(v, 1, keepdims=True) * scale
    var = jnp.sum(centred * centred, 1, keepdims=True) * scale
    return centred * lax.rsqrt(var + EPS) * gain


def kernel(
    rows_n,
    x_ref,
    mask_smem,
    mask_row,
    in_gain,
    wl,
    wlg,
    wr,
    wrg,
    wg,
    mid_gain,
    wo,
    next_gain,
    out_pair,
    out_norm,
    sa,
    d,
    ps,
    pb,
    sc,
    q,
    gate_buf,
    pair_buf,
    sem_a_send,
    sem_a_recv,
    sem_f_send,
    sem_f_recv,
    sem_p_send,
    sem_p_recv,
    sem_c_send,
    sem_c_recv,
):
    r_n = rows_n
    k_n = r_n // 2
    n = 3 * r_n
    b = r_n
    chans = x_ref.shape[1]
    half = chans // 2
    me = lax.axis_index("row")
    c = lax.axis_index("ch")
    core = lax.rem(me, 2)
    slot = me // 2
    per = k_n // GROUPS

    barrier = pltpu.get_barrier_semaphore()

    def greet_own(t, carry):
        pl.semaphore_signal(barrier, inc=1, device_id={"row": lax.rem(me + t, r_n), "ch": c})
        return carry

    def greet_other(t, carry):
        s = lax.rem(slot + t, k_n)
        pl.semaphore_signal(barrier, inc=1, device_id={"row": 2 * s + core, "ch": 1 - c})
        return carry

    lax.fori_loop(1, r_n, greet_own, 0)
    lax.fori_loop(0, k_n, greet_other, 0)

    hl = wl.shape[1]
    p_row, p_col = iota((2 * hl, hl), 0), iota((2 * hl, hl), 1)
    to_left, to_right = one_hot(p_row == 2 * p_col), one_hot(p_row == 2 * p_col + 1)
    w_lin = (dot(to_left, wl[...], 1, 1) + dot(to_right, wr[...], 1, 1)).astype(BF16)
    w_switch = (dot(to_left, wlg[...], 1, 1) + dot(to_right, wrg[...], 1, 1)).astype(BF16)
    for i in range(3):
        normed = normalize(x_ref[i * n : (i + 1) * n].astype(F32), in_gain[...]).astype(BF16)
        lin = dot(w_lin, normed, 1, 1)
        switch = dot(w_switch, normed, 1, 1)
        mask = mask_row[...].astype(F32) * mask_smem[3 * me + i].astype(F32)
        sides = (jax.nn.sigmoid(switch) * lin * mask).astype(BF16)
        for lb in range(3):
            sa[:, lb, i] = sides[:, lb * b : (lb + 1) * b].reshape(hl, 2, b)

    pl.semaphore_wait(barrier, r_n - 1 + k_n)

    group = slot // per

    def send_a(t, carry):
        s = lax.rem(slot + t, k_n)
        pltpu.make_async_remote_copy(
            src_ref=sa.at[s],
            dst_ref=d.at[core, :, slot],
            send_sem=sem_a_send,
            recv_sem=sem_a_recv.at[group],
            device_id={"row": 2 * s + core, "ch": c},
        ).start()
        return carry

    lax.fori_loop(1, k_n, send_a, 0)
    pltpu.make_async_copy(sa.at[slot], d.at[core, :, slot], sem_a_recv.at[group]).start()

    p_row, p_col = iota((2 * r_n, 2 * n), 0), iota((2 * r_n, 2 * n), 1)
    first = (p_row & 1) * n + 3 * (p_row >> 1)
    for j in range(3):
        rows = dot(one_hot(p_col == first + j), x_ref[0 : 2 * n], 1, 0)
        ps[j] = rows.astype(BF16).reshape(r_n, 2, chans)
    p_row, p_col = iota((2 * r_n, n), 0), iota((2 * r_n, n), 1)
    last = x_ref[2 * n : 3 * n]
    rows = dot(one_hot(p_col == 3 * (p_row >> 1) + (p_row & 1)), last, 1, 0)
    ps[3] = rows.astype(BF16).reshape(r_n, 2, chans)
    rows = dot(one_hot(p_col == 3 * (p_row >> 1) + 2), last, 1, 0)
    ps[4] = rows.astype(BF16).reshape(r_n, 2, chans)

    def send_p(t, carry):
        r = lax.rem(me + t, r_n)
        pltpu.make_async_remote_copy(
            src_ref=ps.at[:, r],
            dst_ref=pb.at[:, me],
            send_sem=sem_p_send,
            recv_sem=sem_p_recv,
            device_id={"row": r, "ch": c},
        ).start()
        return carry

    lax.fori_loop(1, r_n, send_p, 0)
    pltpu.make_async_copy(ps.at[:, me], pb.at[:, me], sem_p_recv).start()

    s_row, s_col = iota((n, n), 0), iota((n, n), 1)
    sixth = (s_col * 10923) >> 16
    left_at = 6 * sixth + ((s_col - 6 * sixth) >> 1)
    is_left = (s_col & 1) == 0
    sel_left = [one_hot((s_row == left_at + 3 * h) & is_left) for h in range(2)]
    s_row, s_col = iota((2 * r_n, n), 0), iota((2 * r_n, n), 1)
    in_two = s_row < r_n
    s_two = jnp.where(in_two, s_row, s_row - r_n)
    sel_right = one_hot(
        s_col == 6 * (s_two >> 1) + jnp.where(in_two, 2 * (s_two & 1) + 1, 5)
    )

    other = {"row": 2 * slot + 1 - core, "ch": c}
    for g in range(GROUPS):
        part = d.at[core, :, g * per : (g + 1) * per]
        pltpu.make_async_copy(part, part, sem_a_recv.at[g]).wait()
        pltpu.make_async_remote_copy(
            src_ref=part,
            dst_ref=part,
            send_sem=sem_f_send,
            recv_sem=sem_f_recv.at[g],
            device_id=other,
        ).start()
    for g in range(GROUPS):
        part = d.at[1 - core, :, g * per : (g + 1) * per]
        pltpu.make_async_copy(part, part, sem_f_recv.at[g]).wait()

    lefts, rights = [], []
    for lb in range(3):
        acc = dot(sel_left[0], d[0, lb].reshape(2 * n // 2, b), 1, 0)
        acc = acc + dot(sel_left[1], d[1, lb].reshape(2 * n // 2, b), 1, 0)
        lefts.append(acc.astype(BF16))
        rights.append(dot(sel_right, d[core, lb].reshape(n, b), 1, 0).astype(BF16))
    triangle = dot(jnp.concatenate(rights, 1), jnp.concatenate(lefts, 1), 1, 1)
    upper, lower = triangle[:r_n], triangle[r_n:]
    for ib in range(3):
        sc[ib] = upper[:, ib * b : (ib + 1) * b].astype(BF16).reshape(k_n, 2, b)
    odd = (iota((r_n, b), 0) & 1) == 1
    sc[3] = jnp.where(odd, lower[:, b : 2 * b], lower[:, :b]).astype(BF16).reshape(k_n, 2, b)
    sc[4] = lower[:, 2 * b :].astype(BF16).reshape(k_n, 2, b)

    k_me = c * k_n + slot

    def send_c(t, carry):
        s = lax.rem(slot + t, k_n)
        pltpu.make_async_remote_copy(
            src_ref=sc.at[:, s],
            dst_ref=q.at[:, k_me],
            send_sem=sem_c_send.at[0],
            recv_sem=sem_c_recv,
            device_id={"row": 2 * s + core, "ch": c},
        ).start()
        return carry

    def send_c_other(t, carry):
        s = lax.rem(slot + t, k_n)
        pltpu.make_async_remote_copy(
            src_ref=sc.at[:, s],
            dst_ref=q.at[:, k_me],
            send_sem=sem_c_send.at[1],
            recv_sem=sem_c_recv,
            device_id={"row": 2 * s + core, "ch": 1 - c},
        ).start()
        return carry

    lax.fori_loop(0, k_n, send_c_other, 0)
    lax.fori_loop(1, k_n, send_c, 0)
    pltpu.make_async_copy(sc.at[:, slot], q.at[:, k_me], sem_c_recv).start()

    pltpu.make_async_copy(pb, pb, sem_p_recv).wait()
    s_row, s_col = iota((n, 2 * r_n), 0), iota((n, 2 * r_n), 1)
    sel_two = one_hot(s_row == 3 * (s_col >> 1) + (s_col & 1))
    third = s_row == 3 * (s_col >> 1) + 2
    sel_last = [one_hot(third & ((s_col & 1) == s)) for s in range(2)]
    for j in range(3):
        rest = pb[3 + j // 2].reshape(2 * r_n, chans)
        cells = dot(sel_two, pb[j].reshape(2 * r_n, chans), 1, 0) + dot(sel_last[j % 2], rest, 1, 0)
        pair_buf[j] = cells
        normed = normalize(cells, in_gain[...]).astype(BF16)
        gate_buf[j] = jax.nn.sigmoid(dot(normed, wg[...], 1, 0))

    hidden = wo.shape[0]
    p_row, p_col = iota((2 * hidden, hidden), 0), iota((2 * hidden, hidden), 1)
    twice = (p_row >> 1) == p_col
    gain_col = jnp.sum(jnp.where(twice, mid_gain[...], 0.0), 1, keepdims=True)
    w_twice = dot(one_hot(twice), wo[...], 1, 0)
    even = (iota((2 * hidden, chans), 0) & 1) == 0
    w_out = jnp.concatenate(
        [jnp.where(even, w_twice, 0.0), jnp.where(even, 0.0, w_twice)], 1
    ).astype(BF16)
    gain_all = jnp.broadcast_to(gain_col, (2 * hidden, b))

    pltpu.make_async_copy(q, q, sem_c_recv).wait()

    def total(v):
        t = jnp.sum(v.reshape(2 * hidden // 8, 8, b), 0)
        t = t + pltpu.roll(t, 4, 0)
        t = t + pltpu.roll(t, 2, 0)
        return jnp.broadcast_to(t[None], (2 * hidden // 8, 8, b)).reshape(2 * hidden, b)

    def finish(j, ib, update):
        span = slice(ib * b, (ib + 1) * b)
        new = (pair_buf[j, span] + gate_buf[j, span] * update).astype(BF16)
        values = new.astype(F32)
        normed = normalize(values, next_gain[...])
        second = c == 1
        out_pair[j, span] = jnp.where(second, values[:, half:], values[:, :half]).astype(BF16)
        out_norm[j, span] = jnp.where(second, normed[:, half:], normed[:, :half]).astype(BF16)

    for w in range(5):
        t = q[w].reshape(2 * hidden, b).astype(F32)
        centred = t - total(t) * (1.0 / hidden)
        var = total(centred * centred) * (1.0 / hidden)
        tri = (centred * lax.rsqrt(var + EPS) * gain_all).astype(BF16)
        update = dot(tri, w_out, 0, 0)
        if w < 3:
            finish(0, w, update[:, :chans])
            finish(1, w, update[:, chans:])
        elif w == 3:
            finish(2, 0, update[:, :chans])
            finish(2, 1, update[:, chans:])
        else:
            finish(2, 2, update[:, :chans])

    part = sa.at[0 : k_n - 1]
    pltpu.make_async_copy(part, part, sem_a_send).wait()
    part = d.at[core]
    pltpu.make_async_copy(part, part, sem_f_send).wait()
    part = ps.at[:, 0 : r_n - 1]
    pltpu.make_async_copy(part, part, sem_p_send).wait()
    part = sc.at[:, 0 : k_n - 1]
    pltpu.make_async_copy(part, part, sem_c_send.at[0]).wait()
    pltpu.make_async_copy(sc, sc, sem_c_send.at[1]).wait()


def local(
    r_n,
    pair_rep,
    res_mask,
    in_gain,
    w_left,
    w_left_gate,
    w_right,
    w_right_gate,
    w_gate,
    mid_gain,
    w_out,
    next_gain,
):
    rows, n, chans = pair_rep.shape
    k_n = r_n // 2
    half = chans // 2
    vmem = pl.BlockSpec(memory_space=pltpu.VMEM)
    smem = pl.BlockSpec(memory_space=pltpu.SMEM)
    dma = pltpu.SemaphoreType.DMA
    out = jax.ShapeDtypeStruct((3, n, half), BF16)
    new_pair, new_norm = pl.pallas_call(
        functools.partial(kernel, r_n),
        out_shape=(out, out),
        in_specs=[vmem, smem] + [vmem] * 10,
        out_specs=(vmem, vmem),
        scratch_shapes=[
            pltpu.VMEM((k_n, 3, 3, 2, r_n), BF16),
            pltpu.VMEM((2, 3, k_n, 3, 2, r_n), BF16),
            pltpu.VMEM((5, r_n, 2, chans), BF16),
            pltpu.VMEM((5, r_n, 2, chans), BF16),
            pltpu.VMEM((5, k_n, 2, r_n), BF16),
            pltpu.VMEM((5, r_n, 2, r_n), BF16),
            pltpu.VMEM((3, n, chans), F32),
            pltpu.VMEM((3, n, chans), F32),
            dma,
            dma((GROUPS,)),
            dma,
            dma((GROUPS,)),
            dma,
            dma,
            dma((2,)),
            dma,
        ],
        compiler_params=pltpu.CompilerParams(collective_id=0, has_side_effects=True),
    )(
        pair_rep.reshape(rows * n, chans),
        res_mask,
        res_mask.reshape(1, n),
        in_gain.reshape(1, chans),
        w_left,
        w_left_gate,
        w_right,
        w_right_gate,
        w_gate,
        mid_gain.reshape(1, -1),
        w_out,
        next_gain.reshape(1, chans),
    )
    return jnp.transpose(new_pair, (1, 0, 2)), jnp.transpose(new_norm, (1, 0, 2))


def solution(mesh):
    return jax.shard_map(
        functools.partial(local, mesh.shape["row"]),
        mesh=mesh,
        in_specs=(
            P("row", None, None),
            P(),
            P(),
            P(None, "ch"),
            P(None, "ch"),
            P(None, "ch"),
            P(None, "ch"),
            P(),
            P(),
            P(),
            P(),
        ),
        out_specs=(P(None, "row", "ch"), P(None, "row", "ch")),
        check_vma=False,
    )
```

time: 322 us -> 55.2 us (0.17); the launches traced: 317 us -> 54.8 us
  waiting for transfers between devices: 217 us -> 0 us
  Pallas kernels: 0 us -> 46.7 us
  matrix products: 37 us -> 0 us
  starting transfers between devices: 17.7 us -> 0 us
  between operations: 14.3 us -> 0.66 us
  blocking collectives: 13.3 us -> 0 us
  other arithmetic: 7.41 us -> 0 us
    all_gather x1 -> x0, waiting for transfers between devices: 203 us -> none  [local(): lax.all_gather(left_side, ROW, axis=1, tiled=True)]
    pallas_call x0 -> x1, Pallas kernels: none -> 46.7 us  [local(): pl.pallas_call(functools.partial(kernel, r_n), out_shape=(out, out), in_s...]
    dot_general x7 -> x0, matrix products: 37 us -> none  [the longest x1 29.4 us: batched_rows(): lax.dot_general(first, second, (((2,), (2,)), ((0,), (0,))), preferred_el...]
    all_to_all x3 -> x0, starting transfers between devices: 17.6 us -> none  [the longest x1 11 us: moved_by_axis(): whole = lax.all_to_all(whole, axes[k], k, k, tiled=True)]
    all_to_all x3 -> x0, waiting for transfers between devices: 14.6 us -> none  [the longest x1 8.24 us: moved_by_axis(): whole = lax.all_to_all(whole, axes[k], k, k, tiled=True)]
    all_to_all x1 -> x0, blocking collectives: 6.79 us -> none  [moved_by_axis(): whole = lax.all_to_all(whole, axes[k], k, k, tiled=True)]
    unnamed x9 -> x16, local copies, waits for them, and re-layouts: 0.21 us -> 6.93 us
    psum x1 -> x0, blocking collectives: 6.48 us -> none  [packed_total(): so_far = lax.psum(vector, axis)]
  transfers between devices with their start and end apart: 4 -> 0, of which waited for: 4 -> 0; matrix products, arithmetic and copies ran while one was open for 4% -> 0% of each run, Pallas kernels for 0% -> 0%
where the time goes in v1:
time: 55.2 us; the launch traced here: 54.8 us
  Pallas kernels  46.7 us (85%)
  local copies, waits for them, and re-layouts  7.5 us (14%)
  between operations  0.66 us (1%)
    pallas_call x1, Pallas kernels, local(): pl.pallas_call(functools.partial(kernel, r_n), out_shape=(out, out), in_s...  46.7 us
    unnamed x16, local copies, waits for them, and re-layouts  6.93 us

profile of v1, /device:TPU:1, one launch (start us, length us, event | category | flops | bytes accessed | tf_op | source)
XLA Modules:
  0.0 54.8 jit_solution(16502764027875214655)
XLA Ops:
  0.6 0.0 copy-start.4
  0.6 0.7 %copy-done.4 = s32[384]{0:T(512)S(1)} copy-done((s32[384]{0:T(512)S(1)}, s32[384]{0:T(512)}, u32[]{:S(2)}) %copy-start.4) | copy-done | bytes 1560
  1.3 0.6 %reshape.20.mask_row = s32[1,384]{1,0:T(1,128)} reshape(s32[384]{0:T(512)S(1)} %copy-done.4) | data formatting | bytes 3072 | tf_op jit(solution)/shard_map/reshape | solution.py:335
  1.9 0.0 copy-start.1
  1.9 1.4 %copy.13.wl = bf16[128,64]{1,0:T(8,128)(2,1)} copy(bf16[128,64]{0,1:T(8,128)(2,1)} %param.14) | data formatting | bytes 32768 | tf_op args[3]
  3.3 0.0 copy-done.1
  3.3 0.0 copy-start.2
  3.3 0.7 %copy.14.wlg = bf16[128,64]{1,0:T(8,128)(2,1)} copy(bf16[128,64]{0,1:T(8,128)(2,1)S(1)} %copy-done.1) | data formatting | bytes 32768 | tf_op args[4]
  4.1 0.0 copy-done.2
  4.1 0.0 copy-start.3
  4.1 0.7 %copy.15.wr = bf16[128,64]{1,0:T(8,128)(2,1)} copy(bf16[128,64]{0,1:T(8,128)(2,1)S(1)} %copy-done.2) | data formatting | bytes 32768 | tf_op args[5]
  4.8 0.0 copy-done.3
  4.8 0.7 %copy.16.wrg = bf16[128,64]{1,0:T(8,128)(2,1)} copy(bf16[128,64]{0,1:T(8,128)(2,1)S(1)} %copy-done.3) | data formatting | bytes 32768 | tf_op args[6]
  5.5 46.7 %shard_map.122 = (bf16[3,384,64]{2,1,0:T(8,128)(2,1)}, bf16[3,384,64]{2,1,0:T(8,128)(2,1)}) custom-call(bf16[1152,128]{1,0:T(8,128)(2,1)} %bitcast.8, s32[384]{0:T(512)} %mask_smem.1, s32[1,384]{1,0:T(1,128)} %reshape.20.mask_row, f32[1,128]{1,0:T(1,128)} %bitcast.9, bf16[128,64]{1,0:T(8,128)(2,1)} %copy.13.wl, bf16[128,64]{1,0:T(8,128)(2,1)} %copy.14.wlg, ...), custom_call_target="tpu_custom_call" | custom-call | tf_op jit(solution)/shard_map/pallas_call | solution.py:308
  52.2 0.0 copy-start
  52.2 1.8 %copy.17 = bf16[384,3,64]{0,2,1:T(8,128)(2,1)} copy(bf16[384,3,64]{2,0,1:T(8,128)(2,1)} %bitcast.7) | data formatting | bytes 294912
  54.0 0.0 copy-done
  54.0 0.8 %copy.18 = bf16[384,3,64]{0,2,1:T(8,128)(2,1)} copy(bf16[384,3,64]{2,0,1:T(8,128)(2,1)S(1)} %bitcast.6) | data formatting | bytes 294912
Async XLA Ops:
  0.6 0.7 %copy-start.4 = (s32[384]{0:T(512)S(1)}, s32[384]{0:T(512)}, u32[]{:S(2)}) copy-start(s32[384]{0:T(512)} %mask_smem.1) | copy-start | bytes 4612
  1.9 1.5 %copy-start.1 = (bf16[128,64]{0,1:T(8,128)(2,1)S(1)}, bf16[128,64]{0,1:T(8,128)(2,1)}, u32[]{:S(2)}) copy-start(bf16[128,64]{0,1:T(8,128)(2,1)} %param.15) | copy-start | bytes 49156
  3.3 0.7 %copy-start.2 = (bf16[128,64]{0,1:T(8,128)(2,1)S(1)}, bf16[128,64]{0,1:T(8,128)(2,1)}, u32[]{:S(2)}) copy-start(bf16[128,64]{0,1:T(8,128)(2,1)} %param.16) | copy-start | bytes 49156
  4.1 0.7 %copy-start.3 = (bf16[128,64]{0,1:T(8,128)(2,1)S(1)}, bf16[128,64]{0,1:T(8,128)(2,1)}, u32[]{:S(2)}) copy-start(bf16[128,64]{0,1:T(8,128)(2,1)} %param.17) | copy-start | bytes 49156
  52.2 1.8 %copy-start = (bf16[3,384,64]{2,1,0:T(8,128)(2,1)S(1)}, bf16[3,384,64]{2,1,0:T(8,128)(2,1)}, u32[]{:S(2)}) copy-start(bf16[3,384,64]{2,1,0:T(8,128)(2,1)} %get-tuple-element.5) | copy-start | bytes 442372

commit v2 on v1

--- a/solution.py
+++ b/solution.py
@@ -25,10 +25,16 @@
     return jnp.where(cond, 1.0, 0.0).astype(BF16)
 
 
-def normalize(v, gain):
-    scale = 1.0 / v.shape[1]
-    centred = v - jnp.sum(v, 1, keepdims=True) * scale
-    var = jnp.sum(centred * centred, 1, keepdims=True) * scale
+def to_column(row):
+    size = row.shape[1]
+    diagonal = iota((size, size), 0) == iota((size, size), 1)
+    return jnp.sum(jnp.where(diagonal, row, 0.0), 1, keepdims=True)
+
+
+def normalize(v, gain, along):
+    scale = 1.0 / v.shape[along]
+    centred = v - jnp.sum(v, along, keepdims=True) * scale
+    var = jnp.sum(centred * centred, along, keepdims=True) * scale
     return centred * lax.rsqrt(var + EPS) * gain
 
 
@@ -91,16 +97,16 @@
     lax.fori_loop(1, r_n, greet_own, 0)
     lax.fori_loop(0, k_n, greet_other, 0)
 
-    hl = wl.shape[1]
+    hl = wl.shape[0]
     p_row, p_col = iota((2 * hl, hl), 0), iota((2 * hl, hl), 1)
     to_left, to_right = one_hot(p_row == 2 * p_col), one_hot(p_row == 2 * p_col + 1)
-    w_lin = (dot(to_left, wl[...], 1, 1) + dot(to_right, wr[...], 1, 1)).astype(BF16)
-    w_switch = (dot(to_left, wlg[...], 1, 1) + dot(to_right, wrg[...], 1, 1)).astype(BF16)
+    w_lin = (dot(to_left, wl[...], 1, 0) + dot(to_right, wr[...], 1, 0)).astype(BF16)
+    w_switch = (dot(to_left, wlg[...], 1, 0) + dot(to_right, wrg[...], 1, 0)).astype(BF16)
     for i in range(3):
-        normed = normalize(x_ref[i * n : (i + 1) * n].astype(F32), in_gain[...]).astype(BF16)
+        normed = normalize(x_ref[i * n : (i + 1) * n].astype(F32), in_gain[...], 1).astype(BF16)
         lin = dot(w_lin, normed, 1, 1)
         switch = dot(w_switch, normed, 1, 1)
-        mask = mask_row[...].astype(F32) * mask_smem[3 * me + i].astype(F32)
+        mask = mask_row[...].reshape(1, n).astype(F32) * mask_smem[3 * me + i].astype(F32)
         sides = (jax.nn.sigmoid(switch) * lin * mask).astype(BF16)
         for lb in range(3):
             sa[:, lb, i] = sides[:, lb * b : (lb + 1) * b].reshape(hl, 2, b)
@@ -219,25 +225,26 @@
     pltpu.make_async_copy(sc.at[:, slot], q.at[:, k_me], sem_c_recv).start()
 
     pltpu.make_async_copy(pb, pb, sem_p_recv).wait()
-    s_row, s_col = iota((n, 2 * r_n), 0), iota((n, 2 * r_n), 1)
-    sel_two = one_hot(s_row == 3 * (s_col >> 1) + (s_col & 1))
-    third = s_row == 3 * (s_col >> 1) + 2
-    sel_last = [one_hot(third & ((s_col & 1) == s)) for s in range(2)]
+    s_row, s_col = iota((2 * r_n, n), 0), iota((2 * r_n, n), 1)
+    sel_two = one_hot(s_col == 3 * (s_row >> 1) + (s_row & 1))
+    third = s_col == 3 * (s_row >> 1) + 2
+    sel_last = [one_hot(third & ((s_row & 1) == s)) for s in range(2)]
+    gain_c = to_column(in_gain[...])
     for j in range(3):
         rest = pb[3 + j // 2].reshape(2 * r_n, chans)
-        cells = dot(sel_two, pb[j].reshape(2 * r_n, chans), 1, 0) + dot(sel_last[j % 2], rest, 1, 0)
+        cells = dot(pb[j].reshape(2 * r_n, chans), sel_two, 0, 0) + dot(rest, sel_last[j % 2], 0, 0)
         pair_buf[j] = cells
-        normed = normalize(cells, in_gain[...]).astype(BF16)
-        gate_buf[j] = jax.nn.sigmoid(dot(normed, wg[...], 1, 0))
+        normed = normalize(cells, gain_c, 0).astype(BF16)
+        gate_buf[j] = jax.nn.sigmoid(dot(wg[...], normed, 0, 0))
 
     hidden = wo.shape[0]
     p_row, p_col = iota((2 * hidden, hidden), 0), iota((2 * hidden, hidden), 1)
     twice = (p_row >> 1) == p_col
     gain_col = jnp.sum(jnp.where(twice, mid_gain[...], 0.0), 1, keepdims=True)
-    w_twice = dot(one_hot(twice), wo[...], 1, 0)
-    even = (iota((2 * hidden, chans), 0) & 1) == 0
+    w_twice = dot(wo[...], one_hot(twice), 0, 1)
+    even = (iota((chans, 2 * hidden), 1) & 1) == 0
     w_out = jnp.concatenate(
-        [jnp.where(even, w_twice, 0.0), jnp.where(even, 0.0, w_twice)], 1
+        [jnp.where(even, w_twice, 0.0), jnp.where(even, 0.0, w_twice)], 0
     ).astype(BF16)
     gain_all = jnp.broadcast_to(gain_col, (2 * hidden, b))
 
@@ -249,29 +256,31 @@
         t = t + pltpu.roll(t, 2, 0)
         return jnp.broadcast_to(t[None], (2 * hidden // 8, 8, b)).reshape(2 * hidden, b)
 
+    next_c = to_column(next_gain[...])
+
     def finish(j, ib, update):
         span = slice(ib * b, (ib + 1) * b)
-        new = (pair_buf[j, span] + gate_buf[j, span] * update).astype(BF16)
+        new = (pair_buf[j, :, span] + gate_buf[j, :, span] * update).astype(BF16)
         values = new.astype(F32)
-        normed = normalize(values, next_gain[...])
+        normed = normalize(values, next_c, 0)
         second = c == 1
-        out_pair[j, span] = jnp.where(second, values[:, half:], values[:, :half]).astype(BF16)
-        out_norm[j, span] = jnp.where(second, normed[:, half:], normed[:, :half]).astype(BF16)
+        out_pair[j, :, span] = jnp.where(second, values[half:], values[:half]).astype(BF16)
+        out_norm[j, :, span] = jnp.where(second, normed[half:], normed[:half]).astype(BF16)
 
     for w in range(5):
         t = q[w].reshape(2 * hidden, b).astype(F32)
         centred = t - total(t) * (1.0 / hidden)
         var = total(centred * centred) * (1.0 / hidden)
         tri = (centred * lax.rsqrt(var + EPS) * gain_all).astype(BF16)
-        update = dot(tri, w_out, 0, 0)
+        update = dot(w_out, tri, 1, 0)
         if w < 3:
-            finish(0, w, update[:, :chans])
-            finish(1, w, update[:, chans:])
+            finish(0, w, update[:chans])
+            finish(1, w, update[chans:])
         elif w == 3:
-            finish(2, 0, update[:, :chans])
-            finish(2, 1, update[:, chans:])
+            finish(2, 0, update[:chans])
+            finish(2, 1, update[chans:])
         else:
-            finish(2, 2, update[:, :chans])
+            finish(2, 2, update[:chans])
 
     part = sa.at[0 : k_n - 1]
     pltpu.make_async_copy(part, part, sem_a_send).wait()
@@ -304,7 +313,7 @@
     vmem = pl.BlockSpec(memory_space=pltpu.VMEM)
     smem = pl.BlockSpec(memory_space=pltpu.SMEM)
     dma = pltpu.SemaphoreType.DMA
-    out = jax.ShapeDtypeStruct((3, n, half), BF16)
+    out = jax.ShapeDtypeStruct((3, half, n), BF16)
     new_pair, new_norm = pl.pallas_call(
         functools.partial(kernel, r_n),
         out_shape=(out, out),
@@ -317,8 +326,8 @@
             pltpu.VMEM((5, r_n, 2, chans), BF16),
             pltpu.VMEM((5, k_n, 2, r_n), BF16),
             pltpu.VMEM((5, r_n, 2, r_n), BF16),
-            pltpu.VMEM((3, n, chans), F32),
-            pltpu.VMEM((3, n, chans), F32),
+            pltpu.VMEM((3, chans, n), F32),
+            pltpu.VMEM((3, chans, n), F32),
             dma,
             dma((GROUPS,)),
             dma,
@@ -332,18 +341,18 @@
     )(
         pair_rep.reshape(rows * n, chans),
         res_mask,
-        res_mask.reshape(1, n),
+        res_mask,
         in_gain.reshape(1, chans),
-        w_left,
-        w_left_gate,
-        w_right,
-        w_right_gate,
+        w_left.T,
+        w_left_gate.T,
+        w_right.T,
+        w_right_gate.T,
         w_gate,
         mid_gain.reshape(1, -1),
         w_out,
         next_gain.reshape(1, chans),
     )
-    return jnp.transpose(new_pair, (1, 0, 2)), jnp.transpose(new_norm, (1, 0, 2))
+    return jnp.transpose(new_pair, (2, 0, 1)), jnp.transpose(new_norm, (2, 0, 1))
 
 
 def solution(mesh):

time: 55.2 us -> 47.5 us (0.86)
  local copies, waits for them, and re-layouts: 7.5 us -> 2.29 us
  Pallas kernels: 46.7 us -> 44.4 us
    unnamed x16 -> x4, local copies, waits for them, and re-layouts: 6.93 us -> 2.29 us
    pallas_call x1, Pallas kernels: 46.7 us -> 44.4 us  [local(): pl.pallas_call(functools.partial(kernel, r_n), out_shape=(out, out), in_s...]
    reshape x1 -> x0, local copies, waits for them, and re-layouts: 0.57 us -> none  [local(): res_mask.reshape(1, n)]
where the time goes in v2:
time: 47.5 us; the launch traced here: 47.4 us
  Pallas kernels  44.4 us (93%)
  local copies, waits for them, and re-layouts  2.29 us (5%)
  between operations  0.65 us (1%)
    pallas_call x1, Pallas kernels, local(): pl.pallas_call(functools.partial(kernel, r_n), out_shape=(out, out), in_s...  44.4 us
    unnamed x4, local copies, waits for them, and re-layouts  2.29 us

profile of v2, /device:TPU:1, one launch (start us, length us, event | category | flops | bytes accessed | tf_op | source)
XLA Modules:
  0.0 47.4 jit_solution(17044144680524731646)
XLA Ops:
  0.6 44.4 %shard_map.122 = (bf16[3,64,384]{2,1,0:T(8,128)(2,1)}, bf16[3,64,384]{2,1,0:T(8,128)(2,1)}) custom-call(bf16[1152,128]{1,0:T(8,128)(2,1)} %bitcast.10, s32[384]{0:T(512)} %mask_row.1, s32[384]{0:T(512)} %mask_row.1, f32[1,128]{1,0:T(1,128)} %bitcast.17, bf16[64,128]{1,0:T(8,128)(2,1)} %bitcast.13, bf16[64,128]{1,0:T(8,128)(2,1)} %bitcast.14, ...), custom_call_target="tpu_custom_call" | custom-call | tf_op jit(solution)/shard_map/pallas_call | solution.py:317
  45.1 0.0 copy-start
  45.1 1.6 %copy.15 = bf16[384,3,64]{0,2,1:T(8,128)(2,1)} copy(bf16[384,3,64]{0,2,1:T(8,128)(2,1)} %bitcast.12) | data formatting | bytes 294912
  46.7 0.0 copy-done
  46.7 0.7 %copy.16 = bf16[384,3,64]{0,2,1:T(8,128)(2,1)} copy(bf16[384,3,64]{0,2,1:T(8,128)(2,1)S(1)} %bitcast.11) | data formatting | bytes 294912
Async XLA Ops:
  45.1 1.6 %copy-start = (bf16[3,64,384]{2,1,0:T(8,128)(2,1)S(1)}, bf16[3,64,384]{2,1,0:T(8,128)(2,1)}, u32[]{:S(2)}) copy-start(bf16[3,64,384]{2,1,0:T(8,128)(2,1)} %get-tuple-element.5) | copy-start | bytes 442372

commit v3 on v2

--- a/solution.py
+++ b/solution.py
@@ -40,6 +40,19 @@
 
 def kernel(
     rows_n,
+    x_any,
+    mask_any,
+    in_any,
+    wl_any,
+    wlg_any,
+    wr_any,
+    wrg_any,
+    wg_any,
+    mid_any,
+    wo_any,
+    next_any,
+    out_pair,
+    out_norm,
     x_ref,
     mask_smem,
     mask_row,
@@ -52,8 +65,6 @@
     mid_gain,
     wo,
     next_gain,
-    out_pair,
-    out_norm,
     sa,
     d,
     ps,
@@ -62,6 +73,8 @@
     q,
     gate_buf,
     pair_buf,
+    sem_in,
+    sem_known,
     sem_a_send,
     sem_a_recv,
     sem_f_send,
@@ -82,27 +95,63 @@
     core = lax.rem(me, 2)
     slot = me // 2
     per = k_n // GROUPS
+    x_n = 4 if r_n >= 128 else 2
+    z_n = k_n // (2 * x_n)
+    at_x = lax.rem(slot, x_n)
+    at_y = lax.rem(slot // x_n, 2)
+    at_z = slot // (2 * x_n)
+
+    def chip(u, dy, dx):
+        step = (u + 1) // 2
+        ahead = lax.rem(u + core, 2) == 1
+        z = lax.rem(at_z + jnp.where(ahead, step, z_n - step), z_n)
+        return (z * 2 + lax.rem(at_y + dy, 2)) * x_n + lax.rem(at_x + dx, x_n)
+
+    def tell(sem, u, dy, dx):
+        target = {"row": 2 * chip(u, dy, dx) + core, "ch": c}
+        pl.semaphore_signal(sem, inc=1, device_id=target)
 
     barrier = pltpu.get_barrier_semaphore()
-
-    def greet_own(t, carry):
-        pl.semaphore_signal(barrier, inc=1, device_id={"row": lax.rem(me + t, r_n), "ch": c})
-        return carry
-
-    def greet_other(t, carry):
-        s = lax.rem(slot + t, k_n)
-        pl.semaphore_signal(barrier, inc=1, device_id={"row": 2 * s + core, "ch": 1 - c})
-        return carry
-
-    lax.fori_loop(1, r_n, greet_own, 0)
-    lax.fori_loop(0, k_n, greet_other, 0)
+    other_core = {"row": 2 * slot + 1 - core, "ch": c}
+    other_ch = {"row": me, "ch": 1 - c}
+    for t in range(1, z_n):
+        tell(barrier, z_n - t, 0, 0)
+    for t in range(1, x_n):
+        tell(barrier, 0, 0, t)
+    tell(barrier, 0, 1, 0)
+    pl.semaphore_signal(barrier, inc=1, device_id=other_core)
+    pl.semaphore_signal(barrier, inc=1, device_id=other_ch)
+
+    arrays = (
+        (x_any, x_ref),
+        (wl_any, wl),
+        (wlg_any, wlg),
+        (wr_any, wr),
+        (wrg_any, wrg),
+        (in_any, in_gain),
+        (mask_any, mask_smem),
+        (mask_any, mask_row),
+        (wg_any, wg),
+        (mid_any, mid_gain),
+        (wo_any, wo),
+        (next_any, next_gain),
+    )
+    copies = [
+        pltpu.make_async_copy(src, dst, sem_in.at[i]) for i, (src, dst) in enumerate(arrays)
+    ]
+    for copy in copies:
+        copy.start()
+    for copy in copies[:8]:
+        copy.wait()
 
     hl = wl.shape[0]
     p_row, p_col = iota((2 * hl, hl), 0), iota((2 * hl, hl), 1)
     to_left, to_right = one_hot(p_row == 2 * p_col), one_hot(p_row == 2 * p_col + 1)
     w_lin = (dot(to_left, wl[...], 1, 0) + dot(to_right, wr[...], 1, 0)).astype(BF16)
     w_switch = (dot(to_left, wlg[...], 1, 0) + dot(to_right, wrg[...], 1, 0)).astype(BF16)
-    for i in range(3):
+    group = slot // per
+
+    def project(i):
         normed = normalize(x_ref[i * n : (i + 1) * n].astype(F32), in_gain[...], 1).astype(BF16)
         lin = dot(w_lin, normed, 1, 1)
         switch = dot(w_switch, normed, 1, 1)
@@ -111,12 +160,19 @@
         for lb in range(3):
             sa[:, lb, i] = sides[:, lb * b : (lb + 1) * b].reshape(hl, 2, b)
 
-    pl.semaphore_wait(barrier, r_n - 1 + k_n)
+    project(0)
+    project(1)
+    pl.semaphore_wait(barrier, z_n - 1 + x_n - 1 + 3)
+    for t in range(1, x_n):
+        tell(sem_known.at[0], 0, 0, t)
+    project(2)
+    pl.semaphore_wait(sem_known.at[0], x_n - 1)
+    tell(sem_known.at[1], 0, 1, 0)
 
     group = slot // per
 
-    def send_a(t, carry):
-        s = lax.rem(slot + t, k_n)
+    def send_a(u, dy, dx):
+        s = chip(u, dy, dx)
         pltpu.make_async_remote_copy(
             src_ref=sa.at[s],
             dst_ref=d.at[core, :, slot],
@@ -124,9 +180,20 @@
             recv_sem=sem_a_recv.at[group],
             device_id={"row": 2 * s + core, "ch": c},
         ).start()
+
+    def near(t, carry):
+        send_a(lax.rem(t, z_n), 0, t // z_n)
         return carry
 
-    lax.fori_loop(1, k_n, send_a, 0)
+    def far(t, carry):
+        send_a(lax.rem(t, z_n), 1, t // z_n)
+        return carry
+
+    lax.fori_loop(1, z_n * x_n, near, 0)
+    pl.semaphore_wait(sem_known.at[1], 1)
+    pl.semaphore_signal(sem_known.at[2], inc=1, device_id=other_core)
+    pl.semaphore_signal(sem_known.at[3], inc=1, device_id=other_ch)
+    lax.fori_loop(0, z_n * x_n, far, 0)
     pltpu.make_async_copy(sa.at[slot], d.at[core, :, slot], sem_a_recv.at[group]).start()
 
     p_row, p_col = iota((2 * r_n, 2 * n), 0), iota((2 * r_n, 2 * n), 1)
@@ -141,18 +208,24 @@
     rows = dot(one_hot(p_col == 3 * (p_row >> 1) + 2), last, 1, 0)
     ps[4] = rows.astype(BF16).reshape(r_n, 2, chans)
 
-    def send_p(t, carry):
-        r = lax.rem(me + t, r_n)
-        pltpu.make_async_remote_copy(
-            src_ref=ps.at[:, r],
-            dst_ref=pb.at[:, me],
-            send_sem=sem_p_send,
-            recv_sem=sem_p_recv,
-            device_id={"row": r, "ch": c},
-        ).start()
-        return carry
-
-    lax.fori_loop(1, r_n, send_p, 0)
+    def send_p(to_core):
+        def send(t, carry):
+            s = chip(lax.rem(t, z_n), t // (z_n * x_n), lax.rem(t // z_n, x_n))
+            r = 2 * s + to_core
+            pltpu.make_async_remote_copy(
+                src_ref=ps.at[:, r],
+                dst_ref=pb.at[:, me],
+                send_sem=sem_p_send,
+                recv_sem=sem_p_recv,
+                device_id={"row": r, "ch": c},
+            ).start()
+            return carry
+
+        return send
+
+    pl.semaphore_wait(sem_known.at[2], 1)
+    lax.fori_loop(1, k_n, send_p(core), 0)
+    lax.fori_loop(0, k_n, send_p(1 - core), 0)
     pltpu.make_async_copy(ps.at[:, me], pb.at[:, me], sem_p_recv).start()
 
     s_row, s_col = iota((n, n), 0), iota((n, n), 1)
@@ -167,7 +240,6 @@
         s_col == 6 * (s_two >> 1) + jnp.where(in_two, 2 * (s_two & 1) + 1, 5)
     )
 
-    other = {"row": 2 * slot + 1 - core, "ch": c}
     for g in range(GROUPS):
         part = d.at[core, :, g * per : (g + 1) * per]
         pltpu.make_async_copy(part, part, sem_a_recv.at[g]).wait()
@@ -176,7 +248,7 @@
             dst_ref=part,
             send_sem=sem_f_send,
             recv_sem=sem_f_recv.at[g],
-            device_id=other,
+            device_id=other_core,
         ).start()
     for g in range(GROUPS):
         part = d.at[1 - core, :, g * per : (g + 1) * per]
@@ -198,32 +270,27 @@
 
     k_me = c * k_n + slot
 
-    def send_c(t, carry):
-        s = lax.rem(slot + t, k_n)
-        pltpu.make_async_remote_copy(
-            src_ref=sc.at[:, s],
-            dst_ref=q.at[:, k_me],
-            send_sem=sem_c_send.at[0],
-            recv_sem=sem_c_recv,
-            device_id={"row": 2 * s + core, "ch": c},
-        ).start()
-        return carry
-
-    def send_c_other(t, carry):
-        s = lax.rem(slot + t, k_n)
-        pltpu.make_async_remote_copy(
-            src_ref=sc.at[:, s],
-            dst_ref=q.at[:, k_me],
-            send_sem=sem_c_send.at[1],
-            recv_sem=sem_c_recv,
-            device_id={"row": 2 * s + core, "ch": 1 - c},
-        ).start()
-        return carry
-
-    lax.fori_loop(0, k_n, send_c_other, 0)
-    lax.fori_loop(1, k_n, send_c, 0)
+    def send_c(index, to_ch):
+        def send(t, carry):
+            s = chip(lax.rem(t, z_n), t // (z_n * x_n), lax.rem(t // z_n, x_n))
+            pltpu.make_async_remote_copy(
+                src_ref=sc.at[:, s],
+                dst_ref=q.at[:, k_me],
+                send_sem=sem_c_send.at[index],
+                recv_sem=sem_c_recv,
+                device_id={"row": 2 * s + core, "ch": to_ch},
+            ).start()
+            return carry
+
+        return send
+
+    pl.semaphore_wait(sem_known.at[3], 1)
+    lax.fori_loop(0, k_n, send_c(1, 1 - c), 0)
+    lax.fori_loop(1, k_n, send_c(0, c), 0)
     pltpu.make_async_copy(sc.at[:, slot], q.at[:, k_me], sem_c_recv).start()
 
+    for copy in copies[8:]:
+        copy.wait()
     pltpu.make_async_copy(pb, pb, sem_p_recv).wait()
     s_row, s_col = iota((2 * r_n, n), 0), iota((2 * r_n, n), 1)
     sel_two = one_hot(s_col == 3 * (s_row >> 1) + (s_row & 1))
@@ -310,16 +377,29 @@
     rows, n, chans = pair_rep.shape
     k_n = r_n // 2
     half = chans // 2
+    hl = w_left.shape[1]
     vmem = pl.BlockSpec(memory_space=pltpu.VMEM)
-    smem = pl.BlockSpec(memory_space=pltpu.SMEM)
+    place = pl.BlockSpec(memory_space=pl.ANY)
     dma = pltpu.SemaphoreType.DMA
     out = jax.ShapeDtypeStruct((3, half, n), BF16)
     new_pair, new_norm = pl.pallas_call(
         functools.partial(kernel, r_n),
         out_shape=(out, out),
-        in_specs=[vmem, smem] + [vmem] * 10,
+        in_specs=[place] * 11,
         out_specs=(vmem, vmem),
         scratch_shapes=[
+            pltpu.VMEM((rows * n, chans), BF16),
+            pltpu.SMEM((n,), jnp.int32),
+            pltpu.VMEM((n,), jnp.int32),
+            pltpu.VMEM((1, chans), F32),
+            pltpu.VMEM((hl, chans), BF16),
+            pltpu.VMEM((hl, chans), BF16),
+            pltpu.VMEM((hl, chans), BF16),
+            pltpu.VMEM((hl, chans), BF16),
+            pltpu.VMEM((chans, chans), BF16),
+            pltpu.VMEM((1, r_n), F32),
+            pltpu.VMEM((r_n, chans), BF16),
+            pltpu.VMEM((1, chans), F32),
             pltpu.VMEM((k_n, 3, 3, 2, r_n), BF16),
             pltpu.VMEM((2, 3, k_n, 3, 2, r_n), BF16),
             pltpu.VMEM((5, r_n, 2, chans), BF16),
@@ -328,6 +408,8 @@
             pltpu.VMEM((5, r_n, 2, r_n), BF16),
             pltpu.VMEM((3, chans, n), F32),
             pltpu.VMEM((3, chans, n), F32),
+            dma((12,)),
+            pltpu.SemaphoreType.REGULAR((4,)),
             dma,
             dma((GROUPS,)),
             dma,
@@ -341,7 +423,6 @@
     )(
         pair_rep.reshape(rows * n, chans),
         res_mask,
-        res_mask,
         in_gain.reshape(1, chans),
         w_left.T,
         w_left_gate.T,

time: 47.5 us -> 42.4 us (0.89)
  Pallas kernels: 44.4 us -> 39.4 us
    pallas_call x1, Pallas kernels: 44.4 us -> 39.4 us  [local(): pl.pallas_call(functools.partial(kernel, r_n), out_shape=(out, out), in_s...]
where the time goes in v3:
time: 42.4 us; the launch traced here: 42.3 us
  Pallas kernels  39.4 us (93%)
  local copies, waits for them, and re-layouts  2.29 us (5%)
  between operations  0.65 us (2%)
    pallas_call x1, Pallas kernels, local(): pl.pallas_call(functools.partial(kernel, r_n), out_shape=(out, out), in_s...  39.4 us
    unnamed x4, local copies, waits for them, and re-layouts  2.29 us

profile of v3, /device:TPU:1, one launch (start us, length us, event | category | flops | bytes accessed | tf_op | source)
XLA Modules:
  0.0 42.3 jit_solution(17278798043969710271)
XLA Ops:
  0.6 39.4 %shard_map.122 = (bf16[3,64,384]{2,1,0:T(8,128)(2,1)}, bf16[3,64,384]{2,1,0:T(8,128)(2,1)}) custom-call(bf16[1152,128]{1,0:T(8,128)(2,1)} %bitcast.10, s32[384]{0:T(512)} %mask_any.1, f32[1,128]{1,0:T(1,128)} %bitcast.17, bf16[64,128]{1,0:T(8,128)(2,1)} %bitcast.13, bf16[64,128]{1,0:T(8,128)(2,1)} %bitcast.14, bf16[64,128]{1,0:T(8,128)(2,1)} %bitcast.15, ...), custom_call_target="tpu_custom_call" | custom-call | tf_op jit(solution)/shard_map/pallas_call | solution.py:385
  40.0 0.0 copy-start
  40.0 1.6 %copy.15 = bf16[384,3,64]{0,2,1:T(8,128)(2,1)} copy(bf16[384,3,64]{0,2,1:T(8,128)(2,1)} %bitcast.12) | data formatting | bytes 294912
  41.6 0.0 copy-done
  41.6 0.7 %copy.16 = bf16[384,3,64]{0,2,1:T(8,128)(2,1)} copy(bf16[384,3,64]{0,2,1:T(8,128)(2,1)S(1)} %bitcast.11) | data formatting | bytes 294912
Async XLA Ops:
  40.0 1.6 %copy-start = (bf16[3,64,384]{2,1,0:T(8,128)(2,1)S(1)}, bf16[3,64,384]{2,1,0:T(8,128)(2,1)}, u32[]{:S(2)}) copy-start(bf16[3,64,384]{2,1,0:T(8,128)(2,1)} %get-tuple-element.5) | copy-start | bytes 442372

commit v4 on v3

--- a/solution.py
+++ b/solution.py
@@ -101,24 +101,42 @@
     at_y = lax.rem(slot // x_n, 2)
     at_z = slot // (2 * x_n)
 
-    def chip(u, dy, dx):
-        step = (u + 1) // 2
-        ahead = lax.rem(u + core, 2) == 1
-        z = lax.rem(at_z + jnp.where(ahead, step, z_n - step), z_n)
-        return (z * 2 + lax.rem(at_y + dy, 2)) * x_n + lax.rem(at_x + dx, x_n)
-
-    def tell(sem, u, dy, dx):
-        target = {"row": 2 * chip(u, dy, dx) + core, "ch": c}
-        pl.semaphore_signal(sem, inc=1, device_id=target)
+    ahead = 1 - 2 * core
+    planes = [
+        lax.rem(at_z + z_n + ((u + 1) // 2) * (ahead if u % 2 else -ahead), z_n) * (2 * x_n)
+        for u in range(z_n)
+    ]
+
+    def column(dy, dx):
+        return lax.rem(at_y + dy, 2) * x_n + lax.rem(at_x + dx, x_n)
+
+    here = column(0, 0)
+
+    def tell(sem, chip):
+        pl.semaphore_signal(sem, inc=1, device_id={"row": 2 * chip + core, "ch": c})
+
+    def tell_row(sem):
+        for t in range(1, x_n):
+            tell(sem, planes[0] + column(0, t))
+
+    def all_chips(send, dy, last):
+        def some(t, carry):
+            to = column(dy, x_n - 1 - t)
+            for u in reversed(range(z_n)):
+                send(planes[u] + to)
+            return carry
+
+        lax.fori_loop(0, x_n - 1, some, 0)
+        for u in reversed(range(last, z_n)):
+            send(planes[u] + column(dy, 0))
 
     barrier = pltpu.get_barrier_semaphore()
     other_core = {"row": 2 * slot + 1 - core, "ch": c}
     other_ch = {"row": me, "ch": 1 - c}
-    for t in range(1, z_n):
-        tell(barrier, z_n - t, 0, 0)
-    for t in range(1, x_n):
-        tell(barrier, 0, 0, t)
-    tell(barrier, 0, 1, 0)
+    for u in reversed(range(1, z_n)):
+        tell(barrier, planes[u] + here)
+    tell_row(barrier)
+    tell(barrier, planes[0] + column(1, 0))
     pl.semaphore_signal(barrier, inc=1, device_id=other_core)
     pl.semaphore_signal(barrier, inc=1, device_id=other_ch)
 
@@ -163,16 +181,10 @@
     project(0)
     project(1)
     pl.semaphore_wait(barrier, z_n - 1 + x_n - 1 + 3)
-    for t in range(1, x_n):
-        tell(sem_known.at[0], 0, 0, t)
+    tell_row(sem_known.at[0])
     project(2)
-    pl.semaphore_wait(sem_known.at[0], x_n - 1)
-    tell(sem_known.at[1], 0, 1, 0)
-
-    group = slot // per
-
-    def send_a(u, dy, dx):
-        s = chip(u, dy, dx)
+
+    def send_a(s):
         pltpu.make_async_remote_copy(
             src_ref=sa.at[s],
             dst_ref=d.at[core, :, slot],
@@ -181,19 +193,16 @@
             device_id={"row": 2 * s + core, "ch": c},
         ).start()
 
-    def near(t, carry):
-        send_a(lax.rem(t, z_n), 0, t // z_n)
-        return carry
-
-    def far(t, carry):
-        send_a(lax.rem(t, z_n), 1, t // z_n)
-        return carry
-
-    lax.fori_loop(1, z_n * x_n, near, 0)
+    for u in reversed(range(1, z_n)):
+        send_a(planes[u] + here)
+    pl.semaphore_wait(sem_known.at[0], x_n - 1)
+    tell(sem_known.at[1], planes[0] + column(1, 0))
+
+    all_chips(send_a, 0, z_n)
     pl.semaphore_wait(sem_known.at[1], 1)
     pl.semaphore_signal(sem_known.at[2], inc=1, device_id=other_core)
     pl.semaphore_signal(sem_known.at[3], inc=1, device_id=other_ch)
-    lax.fori_loop(0, z_n * x_n, far, 0)
+    all_chips(send_a, 1, 0)
     pltpu.make_async_copy(sa.at[slot], d.at[core, :, slot], sem_a_recv.at[group]).start()
 
     p_row, p_col = iota((2 * r_n, 2 * n), 0), iota((2 * r_n, 2 * n), 1)
@@ -209,8 +218,7 @@
     ps[4] = rows.astype(BF16).reshape(r_n, 2, chans)
 
     def send_p(to_core):
-        def send(t, carry):
-            s = chip(lax.rem(t, z_n), t // (z_n * x_n), lax.rem(t // z_n, x_n))
+        def send(s):
             r = 2 * s + to_core
             pltpu.make_async_remote_copy(
                 src_ref=ps.at[:, r],
@@ -219,20 +227,22 @@
                 recv_sem=sem_p_recv,
                 device_id={"row": r, "ch": c},
             ).start()
-            return carry
 
         return send
 
     pl.semaphore_wait(sem_known.at[2], 1)
-    lax.fori_loop(1, k_n, send_p(core), 0)
-    lax.fori_loop(0, k_n, send_p(1 - core), 0)
+    all_chips(send_p(core), 1, 0)
+    all_chips(send_p(1 - core), 1, 0)
+    all_chips(send_p(core), 0, 1)
+    all_chips(send_p(1 - core), 0, 0)
     pltpu.make_async_copy(ps.at[:, me], pb.at[:, me], sem_p_recv).start()
 
     s_row, s_col = iota((n, n), 0), iota((n, n), 1)
     sixth = (s_col * 10923) >> 16
     left_at = 6 * sixth + ((s_col - 6 * sixth) >> 1)
     is_left = (s_col & 1) == 0
-    sel_left = [one_hot((s_row == left_at + 3 * h) & is_left) for h in range(2)]
+    sel_own = one_hot((s_row == left_at + 3 * core) & is_left)
+    sel_other = one_hot((s_row == left_at + 3 * (1 - core)) & is_left)
     s_row, s_col = iota((2 * r_n, n), 0), iota((2 * r_n, n), 1)
     in_two = s_row < r_n
     s_two = jnp.where(in_two, s_row, s_row - r_n)
@@ -250,17 +260,18 @@
             recv_sem=sem_f_recv.at[g],
             device_id=other_core,
         ).start()
+
+    owns = [d[core, lb].reshape(n, b) for lb in range(3)]
+    own_left = [dot(sel_own, own, 1, 0) for own in owns]
+    right = jnp.concatenate([dot(sel_right, own, 1, 0).astype(BF16) for own in owns], 1)
     for g in range(GROUPS):
         part = d.at[1 - core, :, g * per : (g + 1) * per]
         pltpu.make_async_copy(part, part, sem_f_recv.at[g]).wait()
-
-    lefts, rights = [], []
+    lefts = []
     for lb in range(3):
-        acc = dot(sel_left[0], d[0, lb].reshape(2 * n // 2, b), 1, 0)
-        acc = acc + dot(sel_left[1], d[1, lb].reshape(2 * n // 2, b), 1, 0)
+        acc = own_left[lb] + dot(sel_other, d[1 - core, lb].reshape(n, b), 1, 0)
         lefts.append(acc.astype(BF16))
-        rights.append(dot(sel_right, d[core, lb].reshape(n, b), 1, 0).astype(BF16))
-    triangle = dot(jnp.concatenate(rights, 1), jnp.concatenate(lefts, 1), 1, 1)
+    triangle = dot(right, jnp.concatenate(lefts, 1), 1, 1)
     upper, lower = triangle[:r_n], triangle[r_n:]
     for ib in range(3):
         sc[ib] = upper[:, ib * b : (ib + 1) * b].astype(BF16).reshape(k_n, 2, b)
@@ -271,8 +282,7 @@
     k_me = c * k_n + slot
 
     def send_c(index, to_ch):
-        def send(t, carry):
-            s = chip(lax.rem(t, z_n), t // (z_n * x_n), lax.rem(t // z_n, x_n))
+        def send(s):
             pltpu.make_async_remote_copy(
                 src_ref=sc.at[:, s],
                 dst_ref=q.at[:, k_me],
@@ -280,13 +290,14 @@
                 recv_sem=sem_c_recv,
                 device_id={"row": 2 * s + core, "ch": to_ch},
             ).start()
-            return carry
 
         return send
 
     pl.semaphore_wait(sem_known.at[3], 1)
-    lax.fori_loop(0, k_n, send_c(1, 1 - c), 0)
-    lax.fori_loop(1, k_n, send_c(0, c), 0)
+    all_chips(send_c(1, 1 - c), 1, 0)
+    all_chips(send_c(1, 1 - c), 0, 0)
+    all_chips(send_c(0, c), 1, 0)
+    all_chips(send_c(0, c), 0, 1)
     pltpu.make_async_copy(sc.at[:, slot], q.at[:, k_me], sem_c_recv).start()
 
     for copy in copies[8:]:
@@ -379,7 +390,7 @@
     half = chans // 2
     hl = w_left.shape[1]
     vmem = pl.BlockSpec(memory_space=pltpu.VMEM)
-    place = pl.BlockSpec(memory_space=pl.ANY)
+    place = pl.BlockSpec(memory_space=pltpu.HBM)
     dma = pltpu.SemaphoreType.DMA
     out = jax.ShapeDtypeStruct((3, half, n), BF16)
     new_pair, new_norm = pl.pallas_call(
@@ -419,19 +430,26 @@
             dma((2,)),
             dma,
         ],
-        compiler_params=pltpu.CompilerParams(collective_id=0, has_side_effects=True),
+        compiler_params=pltpu.CompilerParams(
+            collective_id=0, has_side_effects=True, vmem_limit_bytes=8 * 1024 * 1024
+        ),
     )(
-        pair_rep.reshape(rows * n, chans),
-        res_mask,
-        in_gain.reshape(1, chans),
-        w_left.T,
-        w_left_gate.T,
-        w_right.T,
-        w_right_gate.T,
-        w_gate,
-        mid_gain.reshape(1, -1),
-        w_out,
-        next_gain.reshape(1, chans),
+        *(
+            pltpu.with_memory_space_constraint(a, pltpu.HBM)
+            for a in (
+                pair_rep.reshape(rows * n, chans),
+                res_mask,
+                in_gain.reshape(1, chans),
+                w_left.T,
+                w_left_gate.T,
+                w_right.T,
+                w_right_gate.T,
+                w_gate,
+                mid_gain.reshape(1, -1),
+                w_out,
+                next_gain.reshape(1, chans),
+            )
+        )
     )
     return jnp.transpose(new_pair, (2, 0, 1)), jnp.transpose(new_norm, (2, 0, 1))
 

time: 42.4 us -> 38.5 us (0.908)
  Pallas kernels: 39.4 us -> 36.4 us
  local copies, waits for them, and re-layouts: 2.29 us -> 1.32 us
    pallas_call x1, Pallas kernels: 39.4 us -> 36.4 us  [local(): pl.pallas_call(functools.partial(kernel, r_n), out_shape=(out, out), in_s...]
    unnamed x4 -> x2, local copies, waits for them, and re-layouts: 2.29 us -> 1.32 us
where the time goes in v4:
time: 38.5 us; the launch traced here: 38.4 us
  Pallas kernels  36.4 us (95%)
  local copies, waits for them, and re-layouts  1.32 us (3%)
  between operations  0.64 us (2%)
    pallas_call x1, Pallas kernels, local(): pl.pallas_call(functools.partial(kernel, r_n), out_shape=(out, out), in_s...  36.4 us
    unnamed x2, local copies, waits for them, and re-layouts  1.32 us

profile of v4, /device:TPU:1, one launch (start us, length us, event | category | flops | bytes accessed | tf_op | source)
XLA Modules:
  0.0 38.4 jit_solution(4064530036370146409)
XLA Ops:
  0.6 36.4 %shard_map.122 = (bf16[3,64,384]{2,1,0:T(8,128)(2,1)S(1)}, bf16[3,64,384]{2,1,0:T(8,128)(2,1)S(1)}) custom-call(bf16[1152,128]{1,0:T(8,128)(2,1)} %bitcast.12, s32[384]{0:T(512)} %mask_any.1, f32[1,128]{1,0:T(1,128)} %bitcast.17, bf16[64,128]{1,0:T(8,128)(2,1)} %bitcast.13, bf16[64,128]{1,0:T(8,128)(2,1)} %bitcast.14, bf16[64,128]{1,0:T(8,128)(2,1)} %bitcast.15, ...), custom_call_target="tpu_custom_call" | custom-call | tf_op jit(solution)/shard_map/pallas_call | solution.py:396
  37.1 0.7 %copy.15 = bf16[384,3,64]{0,2,1:T(8,128)(2,1)} copy(bf16[384,3,64]{0,2,1:T(8,128)(2,1)S(1)} %bitcast.11) | data formatting | bytes 294912
  37.7 0.7 %copy.16 = bf16[384,3,64]{0,2,1:T(8,128)(2,1)} copy(bf16[384,3,64]{0,2,1:T(8,128)(2,1)S(1)} %bitcast.10) | data formatting | bytes 294912

commit v5 on v4

--- a/solution.py
+++ b/solution.py
@@ -113,7 +113,7 @@
     here = column(0, 0)
 
     def tell(sem, chip):
-        pl.semaphore_signal(sem, inc=1, device_id={"row": 2 * chip + core, "ch": c})
+        pl.semaphore_signal(sem, inc=1, device_id={"row": 2 * chip + 1, "ch": c})
 
     def tell_row(sem):
         for t in range(1, x_n):
@@ -133,12 +133,22 @@
     barrier = pltpu.get_barrier_semaphore()
     other_core = {"row": 2 * slot + 1 - core, "ch": c}
     other_ch = {"row": me, "ch": 1 - c}
+
+    def tell_other_core(sem):
+        pl.semaphore_signal(sem, inc=1, device_id=other_core)
+
     for u in reversed(range(1, z_n)):
         tell(barrier, planes[u] + here)
     tell_row(barrier)
     tell(barrier, planes[0] + column(1, 0))
-    pl.semaphore_signal(barrier, inc=1, device_id=other_core)
-    pl.semaphore_signal(barrier, inc=1, device_id=other_ch)
+
+    @pl.when(core == 0)
+    def _():
+        tell_other_core(barrier)
+
+    @pl.when(core == 1)
+    def _():
+        pl.semaphore_signal(barrier, inc=1, device_id=other_ch)
 
     arrays = (
         (x_any, x_ref),
@@ -180,8 +190,16 @@
 
     project(0)
     project(1)
-    pl.semaphore_wait(barrier, z_n - 1 + x_n - 1 + 3)
-    tell_row(sem_known.at[0])
+    @pl.when(core == 1)
+    def _():
+        pl.semaphore_wait(barrier, 2 * (z_n + x_n - 1) + 2)
+        tell_row(sem_known.at[0])
+        tell_other_core(barrier)
+
+    @pl.when(core == 0)
+    def _():
+        pl.semaphore_wait(barrier, 1)
+
     project(2)
 
     def send_a(s):
@@ -190,20 +208,36 @@
             dst_ref=d.at[core, :, slot],
             send_sem=sem_a_send,
             recv_sem=sem_a_recv.at[group],
-            device_id={"row": 2 * s + core, "ch": c},
+            device_id={"row": 2 * s + 1 - core, "ch": c},
         ).start()
 
     for u in reversed(range(1, z_n)):
         send_a(planes[u] + here)
-    pl.semaphore_wait(sem_known.at[0], x_n - 1)
-    tell(sem_known.at[1], planes[0] + column(1, 0))
+
+    @pl.when(core == 1)
+    def _():
+        pl.semaphore_wait(sem_known.at[0], x_n - 1)
+        tell(sem_known.at[1], planes[0] + column(1, 0))
+        tell_other_core(sem_known.at[0])
+
+    @pl.when(core == 0)
+    def _():
+        pl.semaphore_wait(sem_known.at[0], 1)
 
     all_chips(send_a, 0, z_n)
-    pl.semaphore_wait(sem_known.at[1], 1)
-    pl.semaphore_signal(sem_known.at[2], inc=1, device_id=other_core)
-    pl.semaphore_signal(sem_known.at[3], inc=1, device_id=other_ch)
+
+    @pl.when(core == 1)
+    def _():
+        pl.semaphore_wait(sem_known.at[1], 1)
+        tell_other_core(sem_known.at[1])
+        pl.semaphore_signal(sem_known.at[2], inc=1, device_id=other_ch)
+
+    @pl.when(core == 0)
+    def _():
+        pl.semaphore_wait(sem_known.at[1], 1)
+
     all_chips(send_a, 1, 0)
-    pltpu.make_async_copy(sa.at[slot], d.at[core, :, slot], sem_a_recv.at[group]).start()
+    send_a(slot)
 
     p_row, p_col = iota((2 * r_n, 2 * n), 0), iota((2 * r_n, 2 * n), 1)
     first = (p_row & 1) * n + 3 * (p_row >> 1)
@@ -217,32 +251,37 @@
     rows = dot(one_hot(p_col == 3 * (p_row >> 1) + 2), last, 1, 0)
     ps[4] = rows.astype(BF16).reshape(r_n, 2, chans)
 
-    def send_p(to_core):
-        def send(s):
-            r = 2 * s + to_core
-            pltpu.make_async_remote_copy(
-                src_ref=ps.at[:, r],
-                dst_ref=pb.at[:, me],
-                send_sem=sem_p_send,
-                recv_sem=sem_p_recv,
-                device_id={"row": r, "ch": c},
-            ).start()
-
-        return send
-
-    pl.semaphore_wait(sem_known.at[2], 1)
-    all_chips(send_p(core), 1, 0)
-    all_chips(send_p(1 - core), 1, 0)
-    all_chips(send_p(core), 0, 1)
-    all_chips(send_p(1 - core), 0, 0)
-    pltpu.make_async_copy(ps.at[:, me], pb.at[:, me], sem_p_recv).start()
+    to_core = lax.rem(c + core, 2)
+
+    def send_p(s):
+        r = 2 * s + to_core
+        pltpu.make_async_remote_copy(
+            src_ref=ps.at[:, r],
+            dst_ref=pb.at[:, core * k_n + slot],
+            send_sem=sem_p_send.at[0],
+            recv_sem=sem_p_recv.at[0],
+            device_id={"row": r, "ch": c},
+        ).start()
+
+    all_chips(send_p, 1, 0)
+    all_chips(send_p, 0, 1)
+
+    @pl.when(c == 0)
+    def _():
+        pltpu.make_async_copy(
+            ps.at[:, me], pb.at[:, core * k_n + slot], sem_p_recv.at[0]
+        ).start()
+
+    @pl.when(c == 1)
+    def _():
+        send_p(slot)
 
     s_row, s_col = iota((n, n), 0), iota((n, n), 1)
     sixth = (s_col * 10923) >> 16
     left_at = 6 * sixth + ((s_col - 6 * sixth) >> 1)
     is_left = (s_col & 1) == 0
-    sel_own = one_hot((s_row == left_at + 3 * core) & is_left)
-    sel_other = one_hot((s_row == left_at + 3 * (1 - core)) & is_left)
+    sel_own = one_hot((s_row == left_at + 3 * (1 - core)) & is_left)
+    sel_other = one_hot((s_row == left_at + 3 * core) & is_left)
     s_row, s_col = iota((2 * r_n, n), 0), iota((2 * r_n, n), 1)
     in_two = s_row < r_n
     s_two = jnp.where(in_two, s_row, s_row - r_n)
@@ -251,7 +290,7 @@
     )
 
     for g in range(GROUPS):
-        part = d.at[core, :, g * per : (g + 1) * per]
+        part = d.at[1 - core, :, g * per : (g + 1) * per]
         pltpu.make_async_copy(part, part, sem_a_recv.at[g]).wait()
         pltpu.make_async_remote_copy(
             src_ref=part,
@@ -261,15 +300,15 @@
             device_id=other_core,
         ).start()
 
-    owns = [d[core, lb].reshape(n, b) for lb in range(3)]
+    owns = [d[1 - core, lb].reshape(n, b) for lb in range(3)]
     own_left = [dot(sel_own, own, 1, 0) for own in owns]
     right = jnp.concatenate([dot(sel_right, own, 1, 0).astype(BF16) for own in owns], 1)
     for g in range(GROUPS):
-        part = d.at[1 - core, :, g * per : (g + 1) * per]
+        part = d.at[core, :, g * per : (g + 1) * per]
         pltpu.make_async_copy(part, part, sem_f_recv.at[g]).wait()
     lefts = []
     for lb in range(3):
-        acc = own_left[lb] + dot(sel_other, d[1 - core, lb].reshape(n, b), 1, 0)
+        acc = own_left[lb] + dot(sel_other, d[core, lb].reshape(n, b), 1, 0)
         lefts.append(acc.astype(BF16))
     triangle = dot(right, jnp.concatenate(lefts, 1), 1, 1)
     upper, lower = triangle[:r_n], triangle[r_n:]
@@ -288,26 +327,46 @@
                 dst_ref=q.at[:, k_me],
                 send_sem=sem_c_send.at[index],
                 recv_sem=sem_c_recv,
-                device_id={"row": 2 * s + core, "ch": to_ch},
+                device_id={"row": 2 * s + 1 - core, "ch": to_ch},
             ).start()
 
         return send
 
-    pl.semaphore_wait(sem_known.at[3], 1)
+
+    @pl.when(core == 1)
+    def _():
+        pl.semaphore_wait(sem_known.at[2], 1)
+        tell_other_core(sem_known.at[2])
+
+    @pl.when(core == 0)
+    def _():
+        pl.semaphore_wait(sem_known.at[2], 1)
+
+    all_chips(send_c(1, 1 - c), 0, 0)
     all_chips(send_c(1, 1 - c), 1, 0)
-    all_chips(send_c(1, 1 - c), 0, 0)
     all_chips(send_c(0, c), 1, 0)
-    all_chips(send_c(0, c), 0, 1)
-    pltpu.make_async_copy(sc.at[:, slot], q.at[:, k_me], sem_c_recv).start()
+    all_chips(send_c(0, c), 0, 0)
 
     for copy in copies[8:]:
         copy.wait()
-    pltpu.make_async_copy(pb, pb, sem_p_recv).wait()
+    mine = pb.at[:, pl.ds(to_core * k_n, k_n)]
+    theirs = pb.at[:, pl.ds((1 - to_core) * k_n, k_n)]
+    pltpu.make_async_copy(mine, mine, sem_p_recv.at[0]).wait()
+    pltpu.make_async_remote_copy(
+        src_ref=mine,
+        dst_ref=mine,
+        send_sem=sem_p_send.at[1],
+        recv_sem=sem_p_recv.at[1],
+        device_id=other_ch,
+    ).start()
     s_row, s_col = iota((2 * r_n, n), 0), iota((2 * r_n, n), 1)
-    sel_two = one_hot(s_col == 3 * (s_row >> 1) + (s_row & 1))
-    third = s_col == 3 * (s_row >> 1) + 2
+    source = s_row >> 1
+    base = jnp.where(source < k_n, 6 * source, 6 * source - 6 * k_n + 3)
+    sel_two = one_hot(s_col == base + (s_row & 1))
+    third = s_col == base + 2
     sel_last = [one_hot(third & ((s_row & 1) == s)) for s in range(2)]
     gain_c = to_column(in_gain[...])
+    pltpu.make_async_copy(theirs, theirs, sem_p_recv.at[1]).wait()
     for j in range(3):
         rest = pb[3 + j // 2].reshape(2 * r_n, chans)
         cells = dot(pb[j].reshape(2 * r_n, chans), sel_two, 0, 0) + dot(rest, sel_last[j % 2], 0, 0)
@@ -324,15 +383,16 @@
     w_out = jnp.concatenate(
         [jnp.where(even, w_twice, 0.0), jnp.where(even, 0.0, w_twice)], 0
     ).astype(BF16)
-    gain_all = jnp.broadcast_to(gain_col, (2 * hidden, b))
+    gain_all = jnp.broadcast_to(gain_col, (2 * hidden, b)).reshape(2 * hidden // 8, 8, b)
 
     pltpu.make_async_copy(q, q, sem_c_recv).wait()
 
-    def total(v):
-        t = jnp.sum(v.reshape(2 * hidden // 8, 8, b), 0)
+    tiles = 2 * hidden // 8
+
+    def mean(v):
+        t = jnp.sum(v, 0)
         t = t + pltpu.roll(t, 4, 0)
-        t = t + pltpu.roll(t, 2, 0)
-        return jnp.broadcast_to(t[None], (2 * hidden // 8, 8, b)).reshape(2 * hidden, b)
+        return (t + pltpu.roll(t, 2, 0)) * (1.0 / hidden)
 
     next_c = to_column(next_gain[...])
 
@@ -346,10 +406,10 @@
         out_norm[j, :, span] = jnp.where(second, normed[half:], normed[:half]).astype(BF16)
 
     for w in range(5):
-        t = q[w].reshape(2 * hidden, b).astype(F32)
-        centred = t - total(t) * (1.0 / hidden)
-        var = total(centred * centred) * (1.0 / hidden)
-        tri = (centred * lax.rsqrt(var + EPS) * gain_all).astype(BF16)
+        t = q[w].reshape(2 * hidden, b).astype(F32).reshape(tiles, 8, b)
+        centred = t - mean(t)[None]
+        scale = lax.rsqrt(mean(centred * centred) + EPS)[None]
+        tri = (centred * scale * gain_all).astype(BF16).reshape(2 * hidden, b)
         update = dot(w_out, tri, 1, 0)
         if w < 3:
             finish(0, w, update[:chans])
@@ -360,14 +420,22 @@
         else:
             finish(2, 2, update[:chans])
 
-    part = sa.at[0 : k_n - 1]
-    pltpu.make_async_copy(part, part, sem_a_send).wait()
-    part = d.at[core]
+    pltpu.make_async_copy(sa, sa, sem_a_send).wait()
+    part = d.at[1 - core]
     pltpu.make_async_copy(part, part, sem_f_send).wait()
-    part = ps.at[:, 0 : r_n - 1]
-    pltpu.make_async_copy(part, part, sem_p_send).wait()
-    part = sc.at[:, 0 : k_n - 1]
-    pltpu.make_async_copy(part, part, sem_c_send.at[0]).wait()
+
+    @pl.when(c == 0)
+    def _():
+        part = ps.at[:, 0 : k_n - 1]
+        pltpu.make_async_copy(part, part, sem_p_send.at[0]).wait()
+
+    @pl.when(c == 1)
+    def _():
+        part = ps.at[:, 0:k_n]
+        pltpu.make_async_copy(part, part, sem_p_send.at[0]).wait()
+
+    pltpu.make_async_copy(mine, mine, sem_p_send.at[1]).wait()
+    pltpu.make_async_copy(sc, sc, sem_c_send.at[0]).wait()
     pltpu.make_async_copy(sc, sc, sem_c_send.at[1]).wait()
 
 
@@ -420,13 +488,13 @@
             pltpu.VMEM((3, chans, n), F32),
             pltpu.VMEM((3, chans, n), F32),
             dma((12,)),
-            pltpu.SemaphoreType.REGULAR((4,)),
+            pltpu.SemaphoreType.REGULAR((3,)),
             dma,
             dma((GROUPS,)),
             dma,
             dma((GROUPS,)),
-            dma,
-            dma,
+            dma((2,)),
+            dma((2,)),
             dma((2,)),
             dma,
         ],

time: 38.5 us -> 38.4 us (level)
  no operation moved by 1% of the time
where the time goes in v5:
time: 38.4 us; the launch traced here: 38.3 us
  Pallas kernels  36.3 us (95%)
  local copies, waits for them, and re-layouts  1.32 us (3%)
  between operations  0.64 us (2%)
    pallas_call x1, Pallas kernels, local(): pl.pallas_call(functools.partial(kernel, r_n), out_shape=(out, out), in_s...  36.3 us
    unnamed x2, local copies, waits for them, and re-layouts  1.32 us

profile of v5, /device:TPU:1, one launch (start us, length us, event | category | flops | bytes accessed | tf_op | source)
XLA Modules:
  0.0 38.3 jit_solution(14611955803432709409)
XLA Ops:
  0.6 36.3 %shard_map.122 = (bf16[3,64,384]{2,1,0:T(8,128)(2,1)S(1)}, bf16[3,64,384]{2,1,0:T(8,128)(2,1)S(1)}) custom-call(bf16[1152,128]{1,0:T(8,128)(2,1)} %bitcast.12, s32[384]{0:T(512)} %mask_any.1, f32[1,128]{1,0:T(1,128)} %bitcast.17, bf16[64,128]{1,0:T(8,128)(2,1)} %bitcast.13, bf16[64,128]{1,0:T(8,128)(2,1)} %bitcast.14, bf16[64,128]{1,0:T(8,128)(2,1)} %bitcast.15, ...), custom_call_target="tpu_custom_call" | custom-call | tf_op jit(solution)/shard_map/pallas_call | solution.py:464
  36.9 0.7 %copy.15 = bf16[384,3,64]{0,2,1:T(8,128)(2,1)} copy(bf16[384,3,64]{0,2,1:T(8,128)(2,1)S(1)} %bitcast.11) | data formatting | bytes 294912
  37.6 0.7 %copy.16 = bf16[384,3,64]{0,2,1:T(8,128)(2,1)} copy(bf16[384,3,64]{0,2,1:T(8,128)(2,1)S(1)} %bitcast.10) | data formatting | bytes 294912

commit v6 on v5

--- a/solution.py
+++ b/solution.py
@@ -10,7 +10,7 @@
 EPS = 1e-05
 F32 = jnp.float32
 BF16 = jnp.bfloat16
-GROUPS = 4
+GROUPS = 8
 
 
 def dot(a, b, ca, cb):

time: 38.4 us -> 38.5 us (level)
  no operation moved by 1% of the time
where the time goes in v6:
time: 38.5 us; the launch traced here: 38.4 us
  Pallas kernels  36.5 us (95%)
  local copies, waits for them, and re-layouts  1.32 us (3%)
  between operations  0.64 us (2%)
    pallas_call x1, Pallas kernels, local(): pl.pallas_call(functools.partial(kernel, r_n), out_shape=(out, out), in_s...  36.5 us
    unnamed x2, local copies, waits for them, and re-layouts  1.32 us

profile of v6, /device:TPU:1, one launch (start us, length us, event | category | flops | bytes accessed | tf_op | source)
XLA Modules:
  0.0 38.4 jit_solution(9016177272338353428)
XLA Ops:
  0.6 36.5 %shard_map.122 = (bf16[3,64,384]{2,1,0:T(8,128)(2,1)S(1)}, bf16[3,64,384]{2,1,0:T(8,128)(2,1)S(1)}) custom-call(bf16[1152,128]{1,0:T(8,128)(2,1)} %bitcast.12, s32[384]{0:T(512)} %mask_any.1, f32[1,128]{1,0:T(1,128)} %bitcast.17, bf16[64,128]{1,0:T(8,128)(2,1)} %bitcast.13, bf16[64,128]{1,0:T(8,128)(2,1)} %bitcast.14, bf16[64,128]{1,0:T(8,128)(2,1)} %bitcast.15, ...), custom_call_target="tpu_custom_call" | custom-call | tf_op jit(solution)/shard_map/pallas_call | solution.py:464
  37.1 0.7 %copy.15 = bf16[384,3,64]{0,2,1:T(8,128)(2,1)} copy(bf16[384,3,64]{0,2,1:T(8,128)(2,1)S(1)} %bitcast.11) | data formatting | bytes 294912
  37.8 0.7 %copy.16 = bf16[384,3,64]{0,2,1:T(8,128)(2,1)} copy(bf16[384,3,64]{0,2,1:T(8,128)(2,1)S(1)} %bitcast.10) | data formatting | bytes 294912
